TPU v7x, 128 devices: a whole 4x4x4 slice. The times are simulated.
128 devices in a mesh: scan: 16 (over z_lo, x, core), tgt: 8 (over y, z_hi).
Axes of the slice: x: 4, y: 4, z: 4 (z_hi: 2, z_lo: 2; z = z_hi * 2 + z_lo), core: 2. Of those that a mesh axis runs over, the one named last changes fastest.
Arguments:
- series: bfloat16 [96, 1200, 8192], P('scan', None, 'tgt'), as said below
- seed_index: int32 [512], replicated, may hold values from 0 to 8191
Outputs:
- affinity: bfloat16 [8192, 8192], P('tgt', 'scan')
Inputs may be any that keep to these rules, and one draw needn't show every extreme that they name: No grayordinate's series is constant over the frames of a scan.
All inputs are finite; a program needn't handle non-finite values.
Results may differ from a plain program's by a relative error of at most 0.0034.
Values may be sent and summed in bfloat16 or wider, within the bound.
A program may use at most 128 MiB of HBM per device.

v0:
```python
import jax
import jax.numpy as jnp
from jax import lax
from jax.sharding import PartitionSpec as P

epsilon = 1e-06
clip_level = 0.95


def fisher_map(values):
    clipped = jnp.clip(values, -clip_level, clip_level)
    return 0.5 * jnp.log((1.0 + clipped) / (1.0 - clipped))


def normalize_columns(profile):
    center = jnp.mean(profile, axis=0)
    deviate = profile - center
    spread = jnp.mean(deviate * deviate, axis=0)
    return (deviate * lax.rsqrt(spread + epsilon)).astype(jnp.bfloat16)


def body(series, seed_index):
    frame_count = series.shape[1]
    local_width = series.shape[2]
    seed_count = seed_index.shape[0]
    tgt_size = lax.axis_size("tgt")
    scan_size = lax.axis_size("scan")
    whole_width = local_width * tgt_size
    first_col = lax.axis_index("tgt") * local_width
    local_seed = seed_index - first_col
    inside = (local_seed >= 0) & (local_seed < local_width)
    safe_seed = jnp.clip(local_seed, 0, local_width - 1)
    values = series.astype(jnp.float32)
    center = jnp.mean(values, axis=1, keepdims=True)
    deviate = values - center
    spread = jnp.mean(deviate * deviate, axis=1, keepdims=True)
    standard = (deviate * lax.rsqrt(spread + epsilon)).astype(jnp.bfloat16)
    picked = jnp.take(standard, safe_seed, axis=2)
    picked = jnp.where(inside[None, None, :], picked, jnp.zeros_like(picked))
    seed_cols = lax.psum(picked, "tgt").astype(jnp.float32).astype(jnp.bfloat16)
    correl = (
        jnp.einsum("sfk,sfg->skg", seed_cols, standard, preferred_element_type=jnp.float32)
        / frame_count
    )
    running = jnp.sum(fisher_map(correl), axis=0)
    total = lax.psum(running, "scan")
    row_prof = normalize_columns(total)
    all_prof = lax.all_gather(row_prof, "tgt", axis=1, tiled=True)
    col_width = whole_width // scan_size
    col_prof = lax.dynamic_slice_in_dim(all_prof, lax.axis_index("scan") * col_width, col_width, 1)
    product = jnp.dot(row_prof.T, col_prof, preferred_element_type=jnp.float32)
    return jnp.tanh(product / seed_count).astype(jnp.bfloat16)


def solution(mesh):
    in_specs = (P("scan", None, "tgt"), P())
    out_specs = P("tgt", "scan")
    return jax.shard_map(body, mesh=mesh, in_specs=in_specs, out_specs=out_specs, check_vma=False)
```

profile of v0, /device:TPU:1, one launch (start us, length us, event | category | flops | bytes accessed | tf_op | source)
XLA Modules:
  0.0 716.5 jit_solution(13805646705477381361)
XLA Ops:
  6.5 0.0 all-reduce.3.cloned.1.call-start
  6.5 0.7 compare_and_fusion
  7.2 28.1 %copy.6 = bf16[6,1200,1024]{1,0,2:T(8,128)(2,1)} copy(bf16[6,1200,1024]{2,1,0:T(8,128)(2,1)} %param.2) | data formatting | bytes 29491200 | tf_op args[0]
  35.4 29.1 %convert_reduce_fusion = f32[6,1024]{0,1:T(8,128)S(1)} fusion(bf16[6,1200,1024]{1,0,2:T(8,128)(2,1)} %copy.6), kind=kLoop, calls=%fused_computation.2 | loop fusion | flops 14739456 | bytes 14770176 | tf_op jit(solution)/shard_map/reduce_sum | solution.py:34
  64.6 0.0 copy-done
  64.6 14.9 %fusion.2 = f32[6,1024]{0,1:T(8,128)S(1)} fusion(bf16[6,1200,1024]{1,0,2:T(8,128)(2,1)S(1)} %copy-done, f32[6,1024]{0,1:T(8,128)S(1)} %broadcast_multiply_fusion), kind=kLoop, calls=%fused_computation.5 | loop fusion | flops 29485056 | bytes 14794752 | tf_op jit(solution)/shard_map/reduce_sum | solution.py:36
  79.5 0.1 add_rsqrt_fusion
  79.6 10.1 %fusion.3 = bf16[6,1200,1024]{1,0,2:T(8,128)(2,1)} fusion(bf16[6,1200,1024]{1,0,2:T(8,128)(2,1)S(1)} %copy-done, f32[6,1024]{0,1:T(8,128)S(1)} %add_rsqrt_fusion, f32[6,1024]{0,1:T(8,128)S(1)} %broadcast_multiply_fusion), kind=kLoop, calls=%fused_computation.6 | loop fusion | flops 29491200 | bytes 29540352 | tf_op jit(solution)/shard_map/convert_element_type | solution.py:37
  89.7 21.0 %gather_fusion = bf16[512,6,1200]{2,1,0:T(8,128)(2,1)} fusion(bf16[6,1200,1024]{1,0,2:T(8,128)(2,1)} %fusion.3, s32[1024]{0:T(1024)S(1)} %pad_clamp_fusion), kind=kCustom, calls=%fused_computation | custom fusion | bytes 14747648 | tf_op jit(solution)/shard_map/jit(_take)/gather | solution.py:38
  110.7 14.7 %copy.7 = bf16[512,6,1200]{0,2,1:T(8,128)(2,1)} copy(bf16[512,6,1200]{2,1,0:T(8,128)(2,1)} %gather_fusion) | data formatting | bytes 14745600 | tf_op jit(solution)/shard_map/jit(_take)/gather | solution.py:38
  125.3 6.9 select_bitcast_fusion
  132.3 0.0 all-reduce.3.cloned.1.call-update
  132.3 0.2 all-reduce.5.cloned.1.call-start
  132.5 308.2 %all-reduce.3.cloned.1.call-done = bf16[6,1200,512]{2,1,0:T(8,128)(2,1)} async-done(((bf16[6,1200,512]{2,1,0:T(8,128)(2,1)}), bf16[6,1200,512]{2,1,0:T(8,128)(2,1)}) %all-reduce.3.cloned.1.call-update) | async-done | bytes 7372816 | tf_op jit(solution)/shard_map/psum | solution.py:40
  440.7 22.3 %multiply_reduce_fusion = f32[512,1024]{1,0:T(8,128)} fusion(bf16[6,1200,512]{2,1,0:T(8,128)(2,1)} %all-reduce.3.cloned.1.call-done, bf16[6,1200,1024]{1,0,2:T(8,128)(2,1)} %fusion.3), kind=kOutput, calls=%fused_computation.9 | convolution fusion | flops 7571243008 | bytes 24215552 | tf_op jit(solution)/shard_map/sfk,sfg->skg/dot_general | solution.py:42
  463.1 0.0 all-reduce.5.cloned.1.call-update
  463.1 0.0 all-gather.2.cloned.1.call-start
  463.1 127.2 %all-reduce.5.cloned.1.call-done = f32[512,1024]{1,0:T(8,128)} async-done(((f32[512,1024]{1,0:T(8,128)}), f32[512,1024]{1,0:T(8,128)}) %all-reduce.5.cloned.1.call-update) | async-done | bytes 2097168 | tf_op jit(solution)/shard_map/psum | solution.py:46
  590.3 1.7 reduce_sum.48
  592.0 1.8 multiply_reduce_fusion.1
  593.9 2.9 multiply_convert_fusion
  596.8 0.0 all-gather.2.cloned.1.call-update
  596.9 109.9 %all-gather.2.cloned.1.call-done = bf16[512,8192]{1,0:T(8,128)(2,1)} async-done(((bf16[512,1024]{1,0:T(8,128)(2,1)}), bf16[512,8192]{1,0:T(8,128)(2,1)}) %all-gather.2.cloned.1.call-update) | async-done | bytes 8388624 | tf_op jit(solution)/shard_map/all_gather | solution.py:48
  706.8 3.1 tanh_convert_fusion
  (5 shorter events, 0.1 us)
Async XLA Ops:
  6.5 434.2 %all-reduce.3.cloned.1.call-start = ((), (), s32[]{:S(2)}) async-start(), calls=%async_computation | async-start | bytes 14745600 | tf_op jit(solution)/shard_map/psum | solution.py:40
  35.4 29.2 %copy-start = (bf16[6,1200,1024]{1,0,2:T(8,128)(2,1)S(1)}, bf16[6,1200,1024]{1,0,2:T(8,128)(2,1)}, u32[]{:S(2)}) copy-start(bf16[6,1200,1024]{1,0,2:T(8,128)(2,1)} %copy.6) | copy-start | bytes 44236804
  132.3 458.0 %all-reduce.5.cloned.1.call-start = ((), (), s32[]{:S(2)}) async-start(), calls=%async_computation.1 | async-start | bytes 4194304 | tf_op jit(solution)/shard_map/psum | solution.py:46
  463.1 243.7 %all-gather.2.cloned.1.call-start = ((), (), s32[]{:S(2)}) async-start(), calls=%async_computation.2 | async-start | bytes 9437184 | tf_op jit(solution)/shard_map/all_gather | solution.py:48
Sparse Core Ops, SparseCore 0:
  132.4 308.2 all-reduce.2
  463.2 127.0 all-reduce.4
  597.0 109.7 all-gather.1
where the time goes:
time: 718 us; the launch traced here: 716 us
  waiting for transfers between devices  545 us (76%)
  other arithmetic  68.4 us (10%)
  local copies, waits for them, and re-layouts  63.8 us (9%)
  matrix products  25.4 us (4%)
  between operations  13.2 us (2%)
    psum x1, waiting for transfers between devices, body(): seed_cols = lax.psum(picked, 'tgt').astype(jnp.float32).astype(jnp.bfloat16)  308 us
    psum x1, waiting for transfers between devices, body(): total = lax.psum(running, 'scan')  127 us
    all_gather x1, waiting for transfers between devices, body(): all_prof = lax.all_gather(row_prof, 'tgt', axis=1, tiled=True)  110 us
    gather x2, local copies, waits for them, and re-layouts, body(): picked = jnp.take(standard, safe_seed, axis=2)  35.6 us
    reduce_sum x1, other arithmetic, body(): center = jnp.mean(values, axis=1, keepdims=True)  29.1 us
    unnamed x3, local copies, waits for them, and re-layouts  28.2 us
    dot_general x1, matrix products, body(): jnp.einsum('sfk,sfg->skg', seed_cols, standard, preferred_element_type=jn...  22.3 us
    reduce_sum x1, other arithmetic, body(): spread = jnp.mean(deviate * deviate, axis=1, keepdims=True)  14.9 us
  transfers between devices with their start and end apart: 3, of which 3 were waited for; matrix products, arithmetic and copies ran while one was open for 0% of the time, Pallas kernels for 0%

commit v1 on v0

--- a/solution.py
+++ b/solution.py
@@ -5,6 +5,11 @@
 
 epsilon = 1e-06
 clip_level = 0.95
+
+
+def add_all(value, axis):
+    parts = lax.all_gather(value, axis)
+    return jnp.sum(parts, axis=0)
 
 
 def fisher_map(values):
@@ -43,7 +48,7 @@
         / frame_count
     )
     running = jnp.sum(fisher_map(correl), axis=0)
-    total = lax.psum(running, "scan")
+    total = add_all(running, "scan")
     row_prof = normalize_columns(total)
     all_prof = lax.all_gather(row_prof, "tgt", axis=1, tiled=True)
     col_width = whole_width // scan_size

time: 718 us -> 787 us (1.096)
  waiting for transfers between devices: 545 us -> 593 us
  other arithmetic: 68.4 us -> 90.7 us
    all_gather x0 -> x1, waiting for transfers between devices: none -> 176 us  [add_all(): parts = lax.all_gather(value, axis)]
    psum x1 -> x0, waiting for transfers between devices: 127 us -> none  [body(): total = lax.psum(running, 'scan')]
    reduce_sum x1, other arithmetic: 1.74 us -> 15 us  [normalize_columns(): center = jnp.mean(profile, axis=0)]
    reduce_sum x0 -> x1, other arithmetic: none -> 12.1 us  [add_all(): return jnp.sum(parts, axis=0)]
where the time goes in v1:
time: 787 us; the launch traced here: 786 us
  waiting for transfers between devices  593 us (75%)
  other arithmetic  90.7 us (12%)
  local copies, waits for them, and re-layouts  63.8 us (8%)
  matrix products  25.3 us (3%)
  between operations  13.2 us (2%)
    psum x1, waiting for transfers between devices, body(): seed_cols = lax.psum(picked, 'tgt').astype(jnp.float32).astype(jnp.bfloat16)  308 us
    all_gather x1, waiting for transfers between devices, add_all(): parts = lax.all_gather(value, axis)  176 us
    all_gather x1, waiting for transfers between devices, body(): all_prof = lax.all_gather(row_prof, 'tgt', axis=1, tiled=True)  109 us
    gather x2, local copies, waits for them, and re-layouts, body(): picked = jnp.take(standard, safe_seed, axis=2)  35.6 us
    reduce_sum x1, other arithmetic, body(): center = jnp.mean(values, axis=1, keepdims=True)  29.1 us
    unnamed x3, local copies, waits for them, and re-layouts  28.2 us
    dot_general x1, matrix products, body(): jnp.einsum('sfk,sfg->skg', seed_cols, standard, preferred_element_type=jn...  22.2 us
  transfers between devices with their start and end apart: 3, of which 3 were waited for; matrix products, arithmetic and copies ran while one was open for 0% of the time, Pallas kernels for 0%

profile of v1, /device:TPU:1, one launch (start us, length us, event | category | flops | bytes accessed | tf_op | source)
XLA Modules:
  0.0 786.0 jit_solution(1042595827996808843)
XLA Ops:
  6.5 0.7 compare_and_fusion
  7.2 28.1 %copy.6 = bf16[6,1200,1024]{1,0,2:T(8,128)(2,1)} copy(bf16[6,1200,1024]{2,1,0:T(8,128)(2,1)} %param.2) | data formatting | bytes 29491200 | tf_op args[0]
  35.4 29.1 %convert_reduce_fusion = f32[6,1024]{0,1:T(8,128)S(1)} fusion(bf16[6,1200,1024]{1,0,2:T(8,128)(2,1)} %copy.6), kind=kLoop, calls=%fused_computation.2 | loop fusion | flops 14739456 | bytes 14770176 | tf_op jit(solution)/shard_map/reduce_sum | solution.py:39
  64.6 0.0 copy-done
  64.6 14.9 %fusion.2 = f32[6,1024]{0,1:T(8,128)S(1)} fusion(bf16[6,1200,1024]{1,0,2:T(8,128)(2,1)S(1)} %copy-done, f32[6,1024]{0,1:T(8,128)S(1)} %broadcast_multiply_fusion), kind=kLoop, calls=%fused_computation.5 | loop fusion | flops 29485056 | bytes 14794752 | tf_op jit(solution)/shard_map/reduce_sum | solution.py:41
  79.5 0.1 add_rsqrt_fusion
  79.6 10.1 %fusion.3 = bf16[6,1200,1024]{1,0,2:T(8,128)(2,1)} fusion(bf16[6,1200,1024]{1,0,2:T(8,128)(2,1)S(1)} %copy-done, f32[6,1024]{0,1:T(8,128)S(1)} %add_rsqrt_fusion, f32[6,1024]{0,1:T(8,128)S(1)} %broadcast_multiply_fusion), kind=kLoop, calls=%fused_computation.6 | loop fusion | flops 29491200 | bytes 29540352 | tf_op jit(solution)/shard_map/convert_element_type | solution.py:42
  89.7 21.0 %gather_fusion = bf16[512,6,1200]{2,1,0:T(8,128)(2,1)} fusion(bf16[6,1200,1024]{1,0,2:T(8,128)(2,1)} %fusion.3, s32[1024]{0:T(1024)S(1)} %pad_clamp_fusion), kind=kCustom, calls=%fused_computation | custom fusion | bytes 14747648 | tf_op jit(solution)/shard_map/jit(_take)/gather | solution.py:43
  110.7 14.7 %copy.7 = bf16[512,6,1200]{0,2,1:T(8,128)(2,1)} copy(bf16[512,6,1200]{2,1,0:T(8,128)(2,1)} %gather_fusion) | data formatting | bytes 14745600 | tf_op jit(solution)/shard_map/jit(_take)/gather | solution.py:43
  125.3 6.9 select_bitcast_fusion
  132.3 0.0 all-reduce.2.cloned.1.call-update
  132.3 0.2 all-gather.6.cloned.1.call-start
  132.5 308.2 %all-reduce.2.cloned.1.call-done = bf16[6,1200,512]{2,1,0:T(8,128)(2,1)} async-done(((bf16[6,1200,512]{2,1,0:T(8,128)(2,1)}), bf16[6,1200,512]{2,1,0:T(8,128)(2,1)}) %all-reduce.2.cloned.1.call-update) | async-done | bytes 7372816 | tf_op jit(solution)/shard_map/psum | solution.py:45
  440.7 22.2 %multiply_reduce_fusion = f32[512,1024]{1,0:T(8,128)} fusion(bf16[6,1200,512]{2,1,0:T(8,128)(2,1)} %all-reduce.2.cloned.1.call-done, bf16[6,1200,1024]{1,0,2:T(8,128)(2,1)} %fusion.3), kind=kOutput, calls=%fused_computation.9 | convolution fusion | flops 7571243008 | bytes 24215552 | tf_op jit(solution)/shard_map/sfk,sfg->skg/dot_general | solution.py:47
  463.0 0.0 all-gather.6.cloned.1.call-update
  463.0 0.0 all-gather.4.cloned.1.call-start
  463.0 175.5 %all-gather.6.cloned.1.call-done = f32[8192,1024]{1,0:T(8,128)} async-done(((f32[512,1024]{1,0:T(8,128)}), f32[8192,1024]{1,0:T(8,128)}) %all-gather.6.cloned.1.call-update) | async-done | bytes 33554448 | tf_op jit(solution)/shard_map/all_gather | solution.py:11
  638.6 12.1 %reduce_sum.57 = f32[512,1024]{1,0:T(8,128)S(1)} reduce(f32[16,512,1024]{2,1,0:T(8,128)} %bitcast.5, f32[]{:T(128)} %constant.23.clone.1), dimensions={0}, to_apply=%region_4.5 | reduce | flops 7864320 | bytes 35651588 | tf_op jit(solution)/shard_map/reduce_sum | solution.py:12
  650.7 15.0 %reduce_sum.58 = f32[1024]{0:T(1024)S(1)} reduce(f32[8192,1024]{1,0:T(8,128)} %all-gather.6.cloned.1.call-done, f32[]{:T(128)} %constant.23.clone.1), dimensions={0}, to_apply=%region_5.6 | reduce | flops 8387584 | bytes 33558532 | tf_op jit(solution)/shard_map/reduce_sum | solution.py:21
  665.7 0.3 multiply_reduce_fusion.1
  666.0 1.4 multiply_convert_fusion
  667.3 0.0 all-gather.4.cloned.1.call-update
  667.4 109.0 %all-gather.4.cloned.1.call-done = bf16[512,8192]{1,0:T(8,128)(2,1)} async-done(((bf16[512,1024]{1,0:T(8,128)(2,1)}), bf16[512,8192]{1,0:T(8,128)(2,1)}) %all-gather.4.cloned.1.call-update) | async-done | bytes 8388624 | tf_op jit(solution)/shard_map/all_gather | solution.py:53
  776.3 3.1 tanh_convert_fusion
  (6 shorter events, 0.1 us)
Async XLA Ops:
  6.5 434.2 %all-reduce.2.cloned.1.call-start = ((), (), s32[]{:S(2)}) async-start(), calls=%async_computation | async-start | bytes 14745600 | tf_op jit(solution)/shard_map/psum | solution.py:45
  35.4 29.2 %copy-start = (bf16[6,1200,1024]{1,0,2:T(8,128)(2,1)S(1)}, bf16[6,1200,1024]{1,0,2:T(8,128)(2,1)}, u32[]{:S(2)}) copy-start(bf16[6,1200,1024]{1,0,2:T(8,128)(2,1)} %copy.6) | copy-start | bytes 44236804
  132.3 506.3 %all-gather.6.cloned.1.call-start = ((), (), s32[]{:S(2)}) async-start(), calls=%async_computation.2 | async-start | bytes 35651584 | tf_op jit(solution)/shard_map/all_gather | solution.py:11
  463.0 313.3 %all-gather.4.cloned.1.call-start = ((), (), s32[]{:S(2)}) async-start(), calls=%async_computation.1 | async-start | bytes 9437184 | tf_op jit(solution)/shard_map/all_gather | solution.py:53
Sparse Core Ops, SparseCore 0:
  132.4 308.2 all-reduce.1
  463.1 175.4 all-gather.5
  667.5 108.7 all-gather.3
